TPU v7x, 32 devices: a whole 2x2x4 slice. The times are simulated.
32 devices in a mesh: rows: 16 (over z, x, core), cols: 2 (over y).
Axes of the slice: x: 2, y: 2, z: 4, core: 2. Of those that a mesh axis runs over, the one named last changes fastest.
Arguments:
- kernel: float32 [16384, 1536], P('rows', 'cols'), may hold values from -0.15625 to 0.15625
- row_orbitals: float32 [16384, 512], P('rows', 'cols'), may hold values from -1.5 to 1.5
- col_orbitals: float32 [1536, 512], P('cols', 'rows'), may hold values from -1.5 to 1.5
- col_vectors: float32 [1536, 512], P('cols', 'rows'), may hold values from -6 to 6
Outputs:
- exchange: float32 [512, 16384], P('cols', 'rows')
All inputs are finite; a program needn't handle non-finite values.
Results may differ from a plain program's by a relative error of at most 0.0003.
Values sent between devices are 32-bit elements; how exact they have to be, the bound alone decides.
A program may use at most 64 MiB of HBM per device.

v0:
```python
import jax
import jax.numpy as jnp
from jax import lax
from jax.sharding import PartitionSpec as P


def body(kernel, row_orbitals, col_orbitals, col_vectors):
    full_rows = lax.all_gather(row_orbitals, "cols", axis=1, tiled=True)
    full_cols = lax.all_gather(col_orbitals, "rows", axis=1, tiled=True)
    full_vecs = lax.all_gather(col_vectors, "rows", axis=1, tiled=True)
    gram = jnp.dot(
        full_rows, full_cols.T, precision=lax.Precision.HIGHEST, preferred_element_type=jnp.float32
    )
    weighted = kernel * gram
    return lax.psum_scatter(
        -jnp.dot(
            full_vecs.T,
            weighted.T,
            precision=lax.Precision.HIGHEST,
            preferred_element_type=jnp.float32,
        ),
        "cols",
        scatter_dimension=0,
        tiled=True,
    )


def solution(mesh):
    in_specs = (P("rows", "cols"), P("rows", "cols"), P("cols", "rows"), P("cols", "rows"))
    out_specs = P("cols", "rows")
    return jax.shard_map(body, mesh=mesh, in_specs=in_specs, out_specs=out_specs, check_vma=False)
```

profile of v0, /device:TPU:0, one launch (start us, length us, event | category | flops | bytes accessed | tf_op | source)
XLA Modules:
  0.0 175.4 jit_solution(11052527146017626073)
XLA Ops:
  6.5 0.0 all-gather.4.cloned.1.call-start
  6.5 0.7 all-gather.4.cloned.1.call-update
  7.3 0.0 all-gather.6.cloned.1.call-start
  7.3 0.7 all-gather.6.cloned.1.call-update
  8.0 0.0 all-gather.8.cloned.1.call-start
  8.1 0.7 all-gather.8.cloned.1.call-update
  8.7 0.0 reduce-scatter.2.cloned.1.call-start
  8.8 35.9 %all-gather.4.cloned.1.call-done = f32[1024,512]{1,0:T(8,128)} async-done(((f32[1024,256]{1,0:T(8,128)}), f32[1024,512]{1,0:T(8,128)}) %all-gather.4.cloned.1.call-update) | async-done | bytes 2097168 | tf_op jit(solution)/shard_map/all_gather | solution.py:8
  44.7 41.9 %all-gather.6.cloned.1.call-done = f32[768,512]{0,1:T(8,128)} async-done(((f32[768,32]{0,1:T(8,128)}), f32[768,512]{0,1:T(8,128)}) %all-gather.6.cloned.1.call-update) | async-done | bytes 1572880 | tf_op jit(solution)/shard_map/all_gather | solution.py:9
  86.6 7.2 %fusion.4 = f32[1024,768]{1,0:T(8,128)S(1)} fusion(f32[1024,512]{1,0:T(8,128)} %all-gather.4.cloned.1.call-done, f32[768,512]{0,1:T(8,128)} %all-gather.6.cloned.1.call-done), kind=kOutput, calls=%fused_computation.3 | convolution fusion | flops 4831838208 | bytes 6815744 | tf_op jit(solution)/shard_map/dot_general | solution.py:11
  93.9 33.4 %all-gather.8.cloned.1.call-done = f32[768,512]{0,1:T(8,128)} async-done(((f32[768,32]{0,1:T(8,128)}), f32[768,512]{0,1:T(8,128)}) %all-gather.8.cloned.1.call-update) | async-done | bytes 1572880 | tf_op jit(solution)/shard_map/all_gather | solution.py:10
  127.3 8.3 %negate_bitcast_fusion = f32[512,1024]{0,1:T(8,128)} fusion(f32[768,512]{0,1:T(8,128)} %all-gather.8.cloned.1.call-done, f32[1024,768]{1,0:T(8,128)} %param.4, f32[1024,768]{1,0:T(8,128)S(1)} %fusion.4), kind=kOutput, calls=%fused_computation.2 | convolution fusion | flops 4833148928 | bytes 9961472 | tf_op jit(solution)/shard_map/dot_general | solution.py:16
  135.6 0.0 reduce-scatter.2.cloned.1.call-update
  135.6 30.8 %reduce-scatter.2.cloned.1.call-done = f32[256,1024]{0,1:T(8,128)} async-done(((f32[512,1024]{0,1:T(8,128)}), f32[256,1024]{0,1:T(8,128)}) %reduce-scatter.2.cloned.1.call-update) | async-done | bytes 1048592 | tf_op jit(solution)/shard_map/reduce_scatter | solution.py:15
  166.4 2.5 %copy.5 = f32[256,1024]{1,0:T(8,128)} copy(f32[256,1024]{0,1:T(8,128)} %reduce-scatter.2.cloned.1.call-done) | data formatting | bytes 2097152 | tf_op jit(solution)/shard_map/reduce_scatter | solution.py:15
Async XLA Ops:
  6.5 38.2 %all-gather.4.cloned.1.call-start = ((), (), s32[]{:S(2)}) async-start(), calls=%async_computation.1 | async-start | bytes 3145728 | tf_op jit(solution)/shard_map/all_gather | solution.py:8
  7.3 79.4 %all-gather.6.cloned.1.call-start = ((), (), s32[]{:S(2)}) async-start(), calls=%async_computation.2 | async-start | bytes 1671168 | tf_op jit(solution)/shard_map/all_gather | solution.py:9
  8.0 119.3 %all-gather.8.cloned.1.call-start = ((), (), s32[]{:S(2)}) async-start(), calls=%async_computation.3 | async-start | bytes 1671168 | tf_op jit(solution)/shard_map/all_gather | solution.py:10
  8.7 157.6 %reduce-scatter.2.cloned.1.call-start = ((), (), s32[]{:S(2)}) async-start(), calls=%async_computation.4 | async-start | bytes 3145728 | tf_op jit(solution)/shard_map/reduce_scatter | solution.py:15
Sparse Core Ops, SparseCore 0:
  8.9 35.8 all-gather.3
  47.0 39.5 all-gather.5
  88.9 38.2 all-gather.7
  135.7 30.6 reduce-scatter.1
where the time goes:
time: 176 us; the launch traced here: 175 us
  waiting for transfers between devices  144 us (82%)
  matrix products  15.6 us (9%)
  between operations  13.1 us (7%)
  local copies, waits for them, and re-layouts  2.53 us (1%)
    all_gather x1, waiting for transfers between devices, body(): full_cols = lax.all_gather(col_orbitals, 'rows', axis=1, tiled=True)  41.9 us
    all_gather x1, waiting for transfers between devices, body(): full_rows = lax.all_gather(row_orbitals, 'cols', axis=1, tiled=True)  35.9 us
    all_gather x1, waiting for transfers between devices, body(): full_vecs = lax.all_gather(col_vectors, 'rows', axis=1, tiled=True)  33.4 us
    reduce_scatter x1, waiting for transfers between devices, body(): lax.psum_scatter(-jnp.dot(full_vecs.T, weighted.T, precision=lax.Precisio...  30.8 us
    dot_general x1, matrix products, body(): jnp.dot(full_vecs.T, weighted.T, precision=lax.Precision.HIGHEST, preferr...  8.31 us
    dot_general x1, matrix products, body(): jnp.dot(full_rows, full_cols.T, precision=lax.Precision.HIGHEST, preferre...  7.25 us
  transfers between devices with their start and end apart: 4, of which 4 were waited for; matrix products, arithmetic and copies ran while one was open for 4% of the time, Pallas kernels for 0%

commit v1 on v0

--- a/solution.py
+++ b/solution.py
@@ -7,7 +7,12 @@
 def body(kernel, row_orbitals, col_orbitals, col_vectors):
     full_rows = lax.all_gather(row_orbitals, "cols", axis=1, tiled=True)
     full_cols = lax.all_gather(col_orbitals, "rows", axis=1, tiled=True)
-    full_vecs = lax.all_gather(col_vectors, "rows", axis=1, tiled=True)
+    ring = [col_vectors]
+    for hop in range(15):
+        ring.append(lax.ppermute(ring[-1], "rows", [(dev, (dev + 1) % 16) for dev in range(16)]))
+    full_vecs = jnp.roll(
+        jnp.concatenate(ring[::-1], axis=1), (lax.axis_index("rows") + 1) * ring[0].shape[1], axis=1
+    )
     gram = jnp.dot(
         full_rows, full_cols.T, precision=lax.Precision.HIGHEST, preferred_element_type=jnp.float32
     )

time: 176 us -> 197 us (1.12)
  local copies, waits for them, and re-layouts: 2.53 us -> 20.5 us
  waiting for transfers between devices: 144 us -> 147 us
    ppermute x0 -> x15, waiting for transfers between devices: none -> 102 us  [body(): lax.ppermute(ring[-1], 'rows', [(dev, (dev + 1) % 16) for dev in range(16)])]
    all_gather x1, waiting for transfers between devices: 35.9 us -> 0.01 us  [body(): full_rows = lax.all_gather(row_orbitals, 'cols', axis=1, tiled=True)]
    all_gather x1 -> x0, waiting for transfers between devices: 33.4 us -> none  [body(): full_vecs = lax.all_gather(col_vectors, 'rows', axis=1, tiled=True)]
    all_gather x1, waiting for transfers between devices: 41.9 us -> 14.2 us  [body(): full_cols = lax.all_gather(col_orbitals, 'rows', axis=1, tiled=True)]
    unnamed x0 -> x35, local copies, waits for them, and re-layouts: none -> 19.8 us
    reduce_scatter x1 -> x0, local copies, waits for them, and re-layouts: 2.53 us -> none  [body(): lax.psum_scatter(-jnp.dot(full_vecs.T, weighted.T, precision=lax.Precisio...]
  transfers between devices with their start and end apart: 4 -> 18, of which waited for: 4 -> 17; matrix products, arithmetic and copies ran while one was open for 4% -> 10% of each run, Pallas kernels for 0% -> 0%
where the time goes in v1:
time: 197 us
  waiting for transfers between devices  147 us (75%)
  local copies, waits for them, and re-layouts  20.5 us (10%)
  matrix products  15.6 us (8%)
  between operations  13.2 us (7%)
    ppermute x15, waiting for transfers between devices, body(): lax.ppermute(ring[-1], 'rows', [(dev, (dev + 1) % 16) for dev in range(16)])  102 us
    reduce_scatter x1, waiting for transfers between devices, body(): lax.psum_scatter(-jnp.dot(full_vecs.T, weighted.T, precision=lax.Precisio...  30.8 us
    unnamed x35, local copies, waits for them, and re-layouts  19.8 us
    all_gather x1, waiting for transfers between devices, body(): full_cols = lax.all_gather(col_orbitals, 'rows', axis=1, tiled=True)  14.2 us
    dot_general x1, matrix products, body(): jnp.dot(full_vecs.T, weighted.T, precision=lax.Precision.HIGHEST, preferr...  8.05 us
    dot_general x1, matrix products, body(): jnp.dot(full_rows, full_cols.T, precision=lax.Precision.HIGHEST, preferre...  7.54 us
  transfers between devices with their start and end apart: 18, of which 17 were waited for; matrix products, arithmetic and copies ran while one was open for 10% of the time, Pallas kernels for 0%

profile of v1, /device:TPU:0, one launch (start us, length us, event | category | flops | bytes accessed | tf_op | source)
XLA Modules:
  0.0 197.3 jit_solution(2809033979335039797)
XLA Ops:
  6.5 0.7 all-gather.3.cloned.1.call-update
  7.8 7.5 %collective-permute-done = f32[768,32]{0,1:T(8,128)S(1)} collective-permute-done((f32[768,32]{0,1:T(8,128)}, f32[768,32]{0,1:T(8,128)S(1)}, u32[]{:S(2)}, u32[]{:S(2)}) %collective-permute-start) | collective-permute-done | bytes 98336 | tf_op jit(solution)/shard_map/ppermute | solution.py:12
  15.3 6.7 %collective-permute-done.1 = f32[768,32]{0,1:T(8,128)S(1)} collective-permute-done((f32[768,32]{0,1:T(8,128)S(1)}, f32[768,32]{0,1:T(8,128)S(1)}, u32[]{:S(2)}, u32[]{:S(2)}) %collective-permute-start.1) | collective-permute-done | bytes 98336 | tf_op jit(solution)/shard_map/ppermute | solution.py:12
  22.1 6.7 %collective-permute-done.2 = f32[768,32]{0,1:T(8,128)S(1)} collective-permute-done((f32[768,32]{0,1:T(8,128)S(1)}, f32[768,32]{0,1:T(8,128)S(1)}, u32[]{:S(2)}, u32[]{:S(2)}) %collective-permute-start.2) | collective-permute-done | bytes 98336 | tf_op jit(solution)/shard_map/ppermute | solution.py:12
  28.8 6.7 %collective-permute-done.3 = f32[768,32]{0,1:T(8,128)S(1)} collective-permute-done((f32[768,32]{0,1:T(8,128)S(1)}, f32[768,32]{0,1:T(8,128)S(1)}, u32[]{:S(2)}, u32[]{:S(2)}) %collective-permute-start.3) | collective-permute-done | bytes 98336 | tf_op jit(solution)/shard_map/ppermute | solution.py:12
  35.5 6.7 %collective-permute-done.4 = f32[768,32]{0,1:T(8,128)S(1)} collective-permute-done((f32[768,32]{0,1:T(8,128)S(1)}, f32[768,32]{0,1:T(8,128)S(1)}, u32[]{:S(2)}, u32[]{:S(2)}) %collective-permute-start.4) | collective-permute-done | bytes 98336 | tf_op jit(solution)/shard_map/ppermute | solution.py:12
  42.3 6.7 %collective-permute-done.5 = f32[768,32]{0,1:T(8,128)S(1)} collective-permute-done((f32[768,32]{0,1:T(8,128)S(1)}, f32[768,32]{0,1:T(8,128)S(1)}, u32[]{:S(2)}, u32[]{:S(2)}) %collective-permute-start.5) | collective-permute-done | bytes 98336 | tf_op jit(solution)/shard_map/ppermute | solution.py:12
  49.0 6.7 %collective-permute-done.6 = f32[768,32]{0,1:T(8,128)S(1)} collective-permute-done((f32[768,32]{0,1:T(8,128)S(1)}, f32[768,32]{0,1:T(8,128)S(1)}, u32[]{:S(2)}, u32[]{:S(2)}) %collective-permute-start.6) | collective-permute-done | bytes 98336 | tf_op jit(solution)/shard_map/ppermute | solution.py:12
  55.8 6.7 %collective-permute-done.7 = f32[768,32]{0,1:T(8,128)S(1)} collective-permute-done((f32[768,32]{0,1:T(8,128)S(1)}, f32[768,32]{0,1:T(8,128)S(1)}, u32[]{:S(2)}, u32[]{:S(2)}) %collective-permute-start.7) | collective-permute-done | bytes 98336 | tf_op jit(solution)/shard_map/ppermute | solution.py:12
  62.5 6.7 %collective-permute-done.8 = f32[768,32]{0,1:T(8,128)S(1)} collective-permute-done((f32[768,32]{0,1:T(8,128)S(1)}, f32[768,32]{0,1:T(8,128)S(1)}, u32[]{:S(2)}, u32[]{:S(2)}) %collective-permute-start.8) | collective-permute-done | bytes 98336 | tf_op jit(solution)/shard_map/ppermute | solution.py:12
  69.2 6.7 %collective-permute-done.9 = f32[768,32]{0,1:T(8,128)S(1)} collective-permute-done((f32[768,32]{0,1:T(8,128)S(1)}, f32[768,32]{0,1:T(8,128)S(1)}, u32[]{:S(2)}, u32[]{:S(2)}) %collective-permute-start.9) | collective-permute-done | bytes 98336 | tf_op jit(solution)/shard_map/ppermute | solution.py:12
  76.0 6.7 %collective-permute-done.10 = f32[768,32]{0,1:T(8,128)S(1)} collective-permute-done((f32[768,32]{0,1:T(8,128)S(1)}, f32[768,32]{0,1:T(8,128)S(1)}, u32[]{:S(2)}, u32[]{:S(2)}) %collective-permute-start.10) | collective-permute-done | bytes 98336 | tf_op jit(solution)/shard_map/ppermute | solution.py:12
  82.7 6.7 %collective-permute-done.11 = f32[768,32]{0,1:T(8,128)S(1)} collective-permute-done((f32[768,32]{0,1:T(8,128)S(1)}, f32[768,32]{0,1:T(8,128)S(1)}, u32[]{:S(2)}, u32[]{:S(2)}) %collective-permute-start.11) | collective-permute-done | bytes 98336 | tf_op jit(solution)/shard_map/ppermute | solution.py:12
  89.5 6.7 %collective-permute-done.12 = f32[768,32]{0,1:T(8,128)S(1)} collective-permute-done((f32[768,32]{0,1:T(8,128)S(1)}, f32[768,32]{0,1:T(8,128)S(1)}, u32[]{:S(2)}, u32[]{:S(2)}) %collective-permute-start.12) | collective-permute-done | bytes 98336 | tf_op jit(solution)/shard_map/ppermute | solution.py:12
  96.2 6.7 %collective-permute-done.13 = f32[768,32]{0,1:T(8,128)S(1)} collective-permute-done((f32[768,32]{0,1:T(8,128)S(1)}, f32[768,32]{0,1:T(8,128)S(1)}, u32[]{:S(2)}, u32[]{:S(2)}) %collective-permute-start.13) | collective-permute-done | bytes 98336 | tf_op jit(solution)/shard_map/ppermute | solution.py:12
  103.0 6.6 %collective-permute-done.14 = f32[768,32]{0,1:T(8,128)S(1)} collective-permute-done((f32[768,32]{0,1:T(8,128)S(1)}, f32[768,32]{0,1:T(8,128)S(1)}, u32[]{:S(2)}, u32[]{:S(2)}) %collective-permute-start.14) | collective-permute-done | bytes 98336 | tf_op jit(solution)/shard_map/ppermute | solution.py:12
  110.9 0.6 constant_dynamic-update-slice_fusion.29
  113.5 0.6 constant_dynamic-update-slice_fusion.25
  114.8 0.6 constant_dynamic-update-slice_fusion.23
  116.1 0.6 constant_dynamic-update-slice_fusion.21
  116.7 0.6 constant_dynamic-update-slice_fusion.20
  118.6 0.6 constant_dynamic-update-slice_fusion.17
  119.9 0.6 constant_dynamic-update-slice_fusion.15
  121.8 0.6 constant_dynamic-update-slice_fusion.12
  122.5 0.6 constant_dynamic-update-slice_fusion.11
  123.7 0.6 constant_dynamic-update-slice_fusion.9
  125.0 0.6 constant_dynamic-update-slice_fusion.7
  129.5 0.7 constant_dynamic-update-slice_fusion
  130.1 14.2 %all-gather.5.cloned.1.call-done = f32[768,512]{0,1:T(8,128)} async-done(((f32[768,32]{0,1:T(8,128)}), f32[768,512]{0,1:T(8,128)}) %all-gather.5.cloned.1.call-update) | async-done | bytes 1572880 | tf_op jit(solution)/shard_map/all_gather | solution.py:9
  144.4 7.5 %fusion.7 = f32[1024,768]{1,0:T(8,128)S(1)} fusion(f32[1024,512]{1,0:T(8,128)} %all-gather.3.cloned.1.call-done, f32[768,512]{0,1:T(8,128)} %all-gather.5.cloned.1.call-done), kind=kOutput, calls=%fused_computation.37 | convolution fusion | flops 4831838208 | bytes 6815744 | tf_op jit(solution)/shard_map/dot_general | solution.py:16
  151.9 8.0 %fusion.2 = f32[512,1024]{1,0:T(8,128)} fusion(f32[1024,768]{1,0:T(8,128)S(1)} %copy-done, f32[1024,768]{1,0:T(8,128)S(1)} %fusion.7, f32[768,1024]{0,1:T(8,128)} %constant_dynamic-update-slice_fusion, s32[]{:T(128)S(6)} %select_n.14), kind=kOutput, calls=%fused_computation.2 | convolution fusion | flops 4833148928 | bytes 9961476 | tf_op jit(solution)/shard_map/dot_general | solution.py:21
  160.0 30.8 %reduce-scatter.2.cloned.1.call-done = f32[256,1024]{1,0:T(8,128)} async-done(((f32[512,1024]{1,0:T(8,128)}), f32[256,1024]{1,0:T(8,128)}) %reduce-scatter.2.cloned.1.call-update) | async-done | bytes 1048592 | tf_op jit(solution)/shard_map/reduce_scatter | solution.py:20
  (45 shorter events, 13.4 us)
Async XLA Ops:
  6.5 112.7 %copy-start.1 = (f32[768,32]{0,1:T(8,128)S(1)}, f32[768,32]{0,1:T(8,128)}, u32[]{:S(2)}) copy-start(f32[768,32]{0,1:T(8,128)} %param.7) | copy-start | bytes 294916
  6.5 123.6 %all-gather.3.cloned.1.call-start = ((), (), s32[]{:S(2)}) async-start(), calls=%async_computation.1 | async-start | bytes 3145728 | tf_op jit(solution)/shard_map/all_gather | solution.py:8
  7.3 137.1 %all-gather.5.cloned.1.call-start = ((), (), s32[]{:S(2)}) async-start(), calls=%async_computation.2 | async-start | bytes 1671168 | tf_op jit(solution)/shard_map/all_gather | solution.py:9
  7.3 8.0 %collective-permute-start = (f32[768,32]{0,1:T(8,128)}, f32[768,32]{0,1:T(8,128)S(1)}, u32[]{:S(2)}, u32[]{:S(2)}) collective-permute-start(f32[768,32]{0,1:T(8,128)} %param.7), channel_id=1, source_target_pairs={{0,2},{2,4},{4,6},{6,8},{8,10},{10,12},{12,14},{14,16},{16,18},{18... | collective-permute-start | bytes 294920 | tf_op jit(solution)/shard_map/ppermute | solution.py:12
  15.3 6.7 %collective-permute-start.1 = (f32[768,32]{0,1:T(8,128)S(1)}, f32[768,32]{0,1:T(8,128)S(1)}, u32[]{:S(2)}, u32[]{:S(2)}) collective-permute-start(f32[768,32]{0,1:T(8,128)S(1)} %collective-permute-done), channel_id=1, source_target_pairs={{0,2},{2,4},{4,6},{6,8},{8,10},{10,12},{12,14},{14,16},{16,18},{18... | collective-permute-start | bytes 294920 | tf_op jit(solution)/shard_map/ppermute | solution.py:12
  22.1 6.7 %collective-permute-start.2 = (f32[768,32]{0,1:T(8,128)S(1)}, f32[768,32]{0,1:T(8,128)S(1)}, u32[]{:S(2)}, u32[]{:S(2)}) collective-permute-start(f32[768,32]{0,1:T(8,128)S(1)} %collective-permute-done.1), channel_id=1, source_target_pairs={{0,2},{2,4},{4,6},{6,8},{8,10},{10,12},{12,14},{14,16},{16,18},{18... | collective-permute-start | bytes 294920 | tf_op jit(solution)/shard_map/ppermute | solution.py:12
  28.8 6.7 %collective-permute-start.3 = (f32[768,32]{0,1:T(8,128)S(1)}, f32[768,32]{0,1:T(8,128)S(1)}, u32[]{:S(2)}, u32[]{:S(2)}) collective-permute-start(f32[768,32]{0,1:T(8,128)S(1)} %collective-permute-done.2), channel_id=1, source_target_pairs={{0,2},{2,4},{4,6},{6,8},{8,10},{10,12},{12,14},{14,16},{16,18},{18... | collective-permute-start | bytes 294920 | tf_op jit(solution)/shard_map/ppermute | solution.py:12
  35.5 6.7 %collective-permute-start.4 = (f32[768,32]{0,1:T(8,128)S(1)}, f32[768,32]{0,1:T(8,128)S(1)}, u32[]{:S(2)}, u32[]{:S(2)}) collective-permute-start(f32[768,32]{0,1:T(8,128)S(1)} %collective-permute-done.3), channel_id=1, source_target_pairs={{0,2},{2,4},{4,6},{6,8},{8,10},{10,12},{12,14},{14,16},{16,18},{18... | collective-permute-start | bytes 294920 | tf_op jit(solution)/shard_map/ppermute | solution.py:12
  42.3 6.7 %collective-permute-start.5 = (f32[768,32]{0,1:T(8,128)S(1)}, f32[768,32]{0,1:T(8,128)S(1)}, u32[]{:S(2)}, u32[]{:S(2)}) collective-permute-start(f32[768,32]{0,1:T(8,128)S(1)} %collective-permute-done.4), channel_id=1, source_target_pairs={{0,2},{2,4},{4,6},{6,8},{8,10},{10,12},{12,14},{14,16},{16,18},{18... | collective-permute-start | bytes 294920 | tf_op jit(solution)/shard_map/ppermute | solution.py:12
  49.0 6.7 %collective-permute-start.6 = (f32[768,32]{0,1:T(8,128)S(1)}, f32[768,32]{0,1:T(8,128)S(1)}, u32[]{:S(2)}, u32[]{:S(2)}) collective-permute-start(f32[768,32]{0,1:T(8,128)S(1)} %collective-permute-done.5), channel_id=1, source_target_pairs={{0,2},{2,4},{4,6},{6,8},{8,10},{10,12},{12,14},{14,16},{16,18},{18... | collective-permute-start | bytes 294920 | tf_op jit(solution)/shard_map/ppermute | solution.py:12
  55.8 6.7 %collective-permute-start.7 = (f32[768,32]{0,1:T(8,128)S(1)}, f32[768,32]{0,1:T(8,128)S(1)}, u32[]{:S(2)}, u32[]{:S(2)}) collective-permute-start(f32[768,32]{0,1:T(8,128)S(1)} %collective-permute-done.6), channel_id=1, source_target_pairs={{0,2},{2,4},{4,6},{6,8},{8,10},{10,12},{12,14},{14,16},{16,18},{18... | collective-permute-start | bytes 294920 | tf_op jit(solution)/shard_map/ppermute | solution.py:12
  62.5 6.7 %collective-permute-start.8 = (f32[768,32]{0,1:T(8,128)S(1)}, f32[768,32]{0,1:T(8,128)S(1)}, u32[]{:S(2)}, u32[]{:S(2)}) collective-permute-start(f32[768,32]{0,1:T(8,128)S(1)} %collective-permute-done.7), channel_id=1, source_target_pairs={{0,2},{2,4},{4,6},{6,8},{8,10},{10,12},{12,14},{14,16},{16,18},{18... | collective-permute-start | bytes 294920 | tf_op jit(solution)/shard_map/ppermute | solution.py:12
  69.2 6.7 %collective-permute-start.9 = (f32[768,32]{0,1:T(8,128)S(1)}, f32[768,32]{0,1:T(8,128)S(1)}, u32[]{:S(2)}, u32[]{:S(2)}) collective-permute-start(f32[768,32]{0,1:T(8,128)S(1)} %collective-permute-done.8), channel_id=1, source_target_pairs={{0,2},{2,4},{4,6},{6,8},{8,10},{10,12},{12,14},{14,16},{16,18},{18... | collective-permute-start | bytes 294920 | tf_op jit(solution)/shard_map/ppermute | solution.py:12
  76.0 6.7 %collective-permute-start.10 = (f32[768,32]{0,1:T(8,128)S(1)}, f32[768,32]{0,1:T(8,128)S(1)}, u32[]{:S(2)}, u32[]{:S(2)}) collective-permute-start(f32[768,32]{0,1:T(8,128)S(1)} %collective-permute-done.9), channel_id=1, source_target_pairs={{0,2},{2,4},{4,6},{6,8},{8,10},{10,12},{12,14},{14,16},{16,18},{18... | collective-permute-start | bytes 294920 | tf_op jit(solution)/shard_map/ppermute | solution.py:12
  82.7 6.7 %collective-permute-start.11 = (f32[768,32]{0,1:T(8,128)S(1)}, f32[768,32]{0,1:T(8,128)S(1)}, u32[]{:S(2)}, u32[]{:S(2)}) collective-permute-start(f32[768,32]{0,1:T(8,128)S(1)} %collective-permute-done.10), channel_id=1, source_target_pairs={{0,2},{2,4},{4,6},{6,8},{8,10},{10,12},{12,14},{14,16},{16,18},{18... | collective-permute-start | bytes 294920 | tf_op jit(solution)/shard_map/ppermute | solution.py:12
  89.4 6.7 %collective-permute-start.12 = (f32[768,32]{0,1:T(8,128)S(1)}, f32[768,32]{0,1:T(8,128)S(1)}, u32[]{:S(2)}, u32[]{:S(2)}) collective-permute-start(f32[768,32]{0,1:T(8,128)S(1)} %collective-permute-done.11), channel_id=1, source_target_pairs={{0,2},{2,4},{4,6},{6,8},{8,10},{10,12},{12,14},{14,16},{16,18},{18... | collective-permute-start | bytes 294920 | tf_op jit(solution)/shard_map/ppermute | solution.py:12
  96.2 6.7 %collective-permute-start.13 = (f32[768,32]{0,1:T(8,128)S(1)}, f32[768,32]{0,1:T(8,128)S(1)}, u32[]{:S(2)}, u32[]{:S(2)}) collective-permute-start(f32[768,32]{0,1:T(8,128)S(1)} %collective-permute-done.12), channel_id=1, source_target_pairs={{0,2},{2,4},{4,6},{6,8},{8,10},{10,12},{12,14},{14,16},{16,18},{18... | collective-permute-start | bytes 294920 | tf_op jit(solution)/shard_map/ppermute | solution.py:12
  102.9 6.7 %collective-permute-start.14 = (f32[768,32]{0,1:T(8,128)S(1)}, f32[768,32]{0,1:T(8,128)S(1)}, u32[]{:S(2)}, u32[]{:S(2)}) collective-permute-start(f32[768,32]{0,1:T(8,128)S(1)} %collective-permute-done.13), channel_id=1, source_target_pairs={{0,2},{2,4},{4,6},{6,8},{8,10},{10,12},{12,14},{14,16},{16,18},{18... | collective-permute-start | bytes 294920 | tf_op jit(solution)/shard_map/ppermute | solution.py:12
  103.0 87.8 %reduce-scatter.2.cloned.1.call-start = ((), (), s32[]{:S(2)}) async-start(), calls=%async_computation.3 | async-start | bytes 3145728 | tf_op jit(solution)/shard_map/reduce_scatter | solution.py:20
  130.1 21.8 %copy-start = (f32[1024,768]{1,0:T(8,128)S(1)}, f32[1024,768]{1,0:T(8,128)}, u32[]{:S(2)}) copy-start(f32[1024,768]{1,0:T(8,128)} %param.4) | copy-start | bytes 9437188
Sparse Core Ops, SparseCore 0:
  8.9 35.8 all-gather.2
  103.1 41.2 all-gather.4
  160.1 30.6 reduce-scatter.1
